TPU v7x, 512 devices: a whole 4x8x8 slice. The times are simulated.
512 devices in a mesh: dp: 4 (over z_lo, core), ctx: 32 (over z_hi, y), tp: 4 (over x).
Axes of the slice: x: 4, y: 8, z: 8 (z_hi: 4, z_lo: 2; z = z_hi * 2 + z_lo), core: 2. Of those that a mesh axis runs over, the one named last changes fastest.
Arguments:
- queries: bfloat16 [16384, 4096], P(('dp', 'ctx'), 'tp'), parts along dimension 0, may hold values from -40 to 40
- keys: bfloat16 [16384, 4096], P(('dp', 'ctx'), 'tp'), parts along dimension 0, may hold values from -40 to 40
- values: bfloat16 [16384, 4096], P(('dp', 'ctx'), 'tp'), parts along dimension 0, may hold values from -6 to 6
- query_gain: float32 [4096], P('tp'), may hold values from 0.1 to 1.9
- key_gain: float32 [4096], P('tp'), may hold values from 0.1 to 1.9
- block_mask: int32 [32, 32], P('ctx'), may hold values from 0 to 1, as said below
Outputs:
- attended: bfloat16 [16384, 4096], P(('dp', 'ctx'), 'tp'), parts along dimension 0
There are 4 independent parts, one for each index of `dp`. A program takes and returns all parts, laid end to end along the dimension named above; an argument that names none is the same for every part. Nothing has to cross between parts.
Inputs may be any that keep to these rules, and one draw needn't show every extreme that they name: block_mask[i, i] is 1 for every i, and block_mask[i, j] is 0 unless |i - j| is a power of two.
All inputs are finite; a program needn't handle non-finite values.
Results may differ from a plain program's by a relative error of at most 0.011.
Values may be sent and summed in bfloat16 or wider, within the bound.
No kernel may reach another device: no remote copies, remote signals or barrier semaphores. Data moves between devices by JAX's collectives and lax.ppermute only.
A program may use at most 128 MiB of HBM per device.

v0:
```python
import jax
import jax.numpy as jnp
from jax import lax
from jax.sharding import PartitionSpec as P

HEADS = 32
HD = 128
BLOCK = 128
epsilon = 1e-06
floor_score = -1e30


def normalize(raw_rows, total_sq, gain_vec, full_width):
    as_float = raw_rows.astype(jnp.float32)
    factor = lax.rsqrt(total_sq / full_width + epsilon)
    return (as_float * factor[:, None] * gain_vec[None, :]).astype(jnp.bfloat16)


def expand_mask(mask_part, block_len):
    q_blocks, k_blocks = mask_part.shape
    spread_out = jnp.broadcast_to(
        mask_part[:, None, :, None], (q_blocks, block_len, k_blocks, block_len)
    )
    return spread_out.reshape(q_blocks * block_len, k_blocks * block_len) > 0


def local(queries, keys, values, query_gain, key_gain, block_mask):
    tok_rows, row_width = queries.shape
    head_count = row_width // HD
    sq_queries = jnp.sum(jnp.square(queries.astype(jnp.float32)), axis=1)
    sq_keys = jnp.sum(jnp.square(keys.astype(jnp.float32)), axis=1)
    tot_queries, tot_keys = lax.psum((sq_queries, sq_keys), "tp")
    full_width = HEADS * HD
    q_normed = normalize(queries, tot_queries, query_gain, full_width).reshape(
        tok_rows, head_count, HD
    )
    k_normed = normalize(keys, tot_keys, key_gain, full_width).reshape(tok_rows, head_count, HD)
    v_heads = values.reshape(tok_rows, head_count, HD)
    score_scale = HD ** (-0.5)
    key_piece = lax.all_gather(k_normed, "ctx", axis=0, tiled=True)
    value_piece = lax.all_gather(v_heads, "ctx", axis=0, tiled=True)
    run_max = jnp.full((head_count, tok_rows), floor_score, jnp.float32)
    run_acc = jnp.zeros((tok_rows, head_count, HD), jnp.float32)
    allowed = expand_mask(block_mask, BLOCK)[None]
    scores = (
        jnp.einsum("qhd,khd->hqk", q_normed, key_piece, preferred_element_type=jnp.float32)
        * score_scale
    )
    scores = jnp.where(allowed, scores, floor_score)
    new_max = jnp.maximum(run_max, jnp.max(scores, axis=2))
    shrink = jnp.exp(run_max - new_max)
    weights = jnp.where(allowed, jnp.exp(scores - new_max[:, :, None]), 0.0)
    new_sum = jnp.sum(weights, axis=2)
    update = jnp.einsum(
        "hqk,khd->qhd",
        weights.astype(jnp.bfloat16),
        value_piece,
        preferred_element_type=jnp.float32,
    )
    new_acc = run_acc * shrink.T[:, :, None] + update
    result = new_acc / new_sum.T[:, :, None]
    return result.astype(jnp.bfloat16).reshape(tok_rows, row_width)


def solution(mesh):
    in_specs = (
        P(("dp", "ctx"), "tp"),
        P(("dp", "ctx"), "tp"),
        P(("dp", "ctx"), "tp"),
        P("tp"),
        P("tp"),
        P("ctx", None),
    )
    out_specs = P(("dp", "ctx"), "tp")
    return jax.shard_map(local, mesh=mesh, in_specs=in_specs, out_specs=out_specs, check_vma=False)
```

profile of v0, /device:TPU:2, one launch (start us, length us, event | category | flops | bytes accessed | tf_op | source)
XLA Modules:
  0.0 330.6 jit_solution(13819743713990285720)
XLA Ops:
  6.5 0.0 all-gather.3.cloned.1.call-start
  6.5 1.1 copy.10
  7.7 0.2 fusion.21
  7.8 1.1 fusion.18
  8.9 13.6 %all-reduce = (f32[128]{0:T(128)S(1)}, f32[128]{0:T(128)S(1)}) all-reduce(f32[128]{0:T(128)S(1)} %fusion.21, f32[128]{0:T(128)S(1)} %fusion.18), channel_id=1, replica_groups=mesh['dp'=4,'ctx'=32,'tp'=4] {'tp'}, use_global_device_ids=true, to_apply=%region_3.0 | all-reduce | flops 256 | bytes 2048 | tf_op jit(solution)/shard_map/psum | solution.py:32
  22.5 0.9 fusion.23
  23.4 0.8 copy.11
  24.2 0.0 all-gather.3.cloned.1.call-update
  24.3 0.0 all-gather.5.cloned.1.call-start
  24.3 1.8 copy.13
  26.1 0.0 all-gather.5.cloned.1.call-update
  26.2 0.7 compare_bitcast_fusion
  26.8 0.1 broadcast_bitcast_fusion
  26.9 137.1 %all-gather.3.cloned.1.call-done = bf16[4096,8,128]{2,0,1:T(8,128)(2,1)} async-done(((bf16[128,8,128]{2,0,1:T(8,128)(2,1)}), bf16[4096,8,128]{2,0,1:T(8,128)(2,1)}) %all-gather.3.cloned.1.call-update) | async-done | bytes 8388624 | tf_op jit(solution)/shard_map/all_gather | solution.py:40
  164.0 11.7 %fusion = (f32[8,128]{1,0:T(8,128)S(1)}, f32[8,128,4096]{2,1,0:T(8,128)}) fusion(pred[4096]{0:T(1024)(128)(4,1)S(1)} %broadcast_bitcast_fusion, bf16[4096,8,128]{2,0,1:T(8,128)(2,1)} %all-gather.3.cloned.1.call-done, bf16[128,1024]{1,0:T(8,128)(2,1)} %param.6, f32[1024]{0:T(1024)} %param.9, f32[128]{0:T(128)S(1)} %add_rsqrt_fusion.1), kind=kOutput, calls=%fused_computation.2 | convolution fusion | flops 1086848000 | bytes 25440768 | tf_op jit(solution)/shard_map/qhd,khd->hqk/dot_general | solution.py:46
  175.7 8.5 %fusion.1 = f32[8,128]{1,0:T(8,128)S(1)} fusion(f32[8,128,4096]{2,1,0:T(8,128)} %get-tuple-element.10, f32[8,128]{1,0:T(8,128)S(1)} %get-tuple-element.8, pred[4096]{0:T(1024)(128)(4,1)S(1)} %broadcast_bitcast_fusion), kind=kLoop, calls=%fused_computation.3 | loop fusion | flops 20970496 | bytes 16789504 | tf_op jit(solution)/shard_map/reduce_sum | solution.py:53
  184.2 128.0 %all-gather.5.cloned.1.call-done = bf16[4096,8,128]{0,2,1:T(8,128)(2,1)} async-done(((bf16[128,8,128]{0,2,1:T(8,128)(2,1)}), bf16[4096,8,128]{0,2,1:T(8,128)(2,1)}) %all-gather.5.cloned.1.call-update) | async-done | bytes 8388624 | tf_op jit(solution)/shard_map/all_gather | solution.py:41
  312.2 10.6 %fusion.15 = bf16[128,8,128]{0,2,1:T(8,128)(2,1)S(1)} fusion(bf16[4096,8,128]{0,2,1:T(8,128)(2,1)} %all-gather.5.cloned.1.call-done, f32[8,128,4096]{2,1,0:T(8,128)} %get-tuple-element.10, f32[8,128]{1,0:T(8,128)S(1)} %get-tuple-element.8, pred[4096]{0:T(1024)(128)(4,1)S(1)} %broadcast_bitcast_fusion, f32[128,8]{0,1:T(8,128)S(1)} %bitcast.32, ...), kind=kOutput, calls=%fused_computation.10 | convolution fusion | flops 1095106560 | bytes 25444352 | tf_op jit(solution)/shard_map/hqk,khd->qhd/dot_general | solution.py:54
  322.9 0.8 copy.14
  (3 shorter events, 0.0 us)
Async XLA Ops:
  6.5 157.4 %all-gather.3.cloned.1.call-start = ((), (), s32[]{:S(2)}) async-start(), calls=%async_computation | async-start | bytes 8650752 | tf_op jit(solution)/shard_map/all_gather | solution.py:40
  24.3 288.0 %all-gather.5.cloned.1.call-start = ((), (), s32[]{:S(2)}) async-start(), calls=%async_computation.1 | async-start | bytes 8650752 | tf_op jit(solution)/shard_map/all_gather | solution.py:41
Sparse Core Ops, SparseCore 0:
  24.4 139.5 all-gather.2
  167.0 145.1 all-gather.4
where the time goes:
time: 331 us
  waiting for transfers between devices  265 us (80%)
  matrix products  22.3 us (7%)
  blocking collectives  13.6 us (4%)
  between operations  13.4 us (4%)
  other arithmetic  11.3 us (3%)
  local copies, waits for them, and re-layouts  4.67 us (1%)
    all_gather x1, waiting for transfers between devices, local(): key_piece = lax.all_gather(k_normed, 'ctx', axis=0, tiled=True)  137 us
    all_gather x1, waiting for transfers between devices, local(): value_piece = lax.all_gather(v_heads, 'ctx', axis=0, tiled=True)  128 us
    psum x1, blocking collectives, local(): tot_queries, tot_keys = lax.psum((sq_queries, sq_keys), 'tp')  13.6 us
    dot_general x1, matrix products, local(): jnp.einsum('qhd,khd->hqk', q_normed, key_piece, preferred_element_type=jn...  11.7 us
    dot_general x1, matrix products, local(): jnp.einsum('hqk,khd->qhd', weights.astype(jnp.bfloat16), value_piece, pre...  10.6 us
    reduce_sum x1, other arithmetic, local(): new_sum = jnp.sum(weights, axis=2)  8.51 us
  transfers between devices with their start and end apart: 2, of which 2 were waited for; matrix products, arithmetic and copies ran while one was open for 7% of the time, Pallas kernels for 0%

commit v1 on v0

--- a/solution.py
+++ b/solution.py
@@ -38,7 +38,9 @@
     v_heads = values.reshape(tok_rows, head_count, HD)
     score_scale = HD ** (-0.5)
     key_piece = lax.all_gather(k_normed, "ctx", axis=0, tiled=True)
-    value_piece = lax.all_gather(v_heads, "ctx", axis=0, tiled=True)
+    value_piece = jnp.concatenate(
+        lax.all_to_all(jnp.stack([v_heads] * lax.axis_size("ctx")), "ctx", 0, 0), axis=0
+    )
     run_max = jnp.full((head_count, tok_rows), floor_score, jnp.float32)
     run_acc = jnp.zeros((tok_rows, head_count, HD), jnp.float32)
     allowed = expand_mask(block_mask, BLOCK)[None]

time: 331 us -> 463 us (1.40)
  the two profiles are of different devices: /device:TPU:2 before, /device:TPU:24 now
where the time goes in v1:
time: 463 us
  waiting for transfers between devices  381 us (82%)
  matrix products  22.1 us (5%)
  starting transfers between devices  16 us (3%)
  between operations  13.5 us (3%)
  other arithmetic  10.5 us (2%)
  blocking collectives  10.5 us (2%)
  local copies, waits for them, and re-layouts  9.38 us (2%)
    all_gather x1, waiting for transfers between devices, local(): key_piece = lax.all_gather(k_normed, 'ctx', axis=0, tiled=True)  381 us
    all_to_all x1, starting transfers between devices, local(): lax.all_to_all(jnp.stack([v_heads] * lax.axis_size('ctx')), 'ctx', 0, 0)  16 us
    dot_general x1, matrix products, local(): jnp.einsum('qhd,khd->hqk', q_normed, key_piece, preferred_element_type=jn...  11.6 us
    psum x1, blocking collectives, local(): tot_queries, tot_keys = lax.psum((sq_queries, sq_keys), 'tp')  10.5 us
    dot_general x1, matrix products, local(): jnp.einsum('hqk,khd->qhd', weights.astype(jnp.bfloat16), value_piece, pre...  10.5 us
  transfers between devices with their start and end apart: 2, of which 1 were waited for; matrix products, arithmetic and copies ran while one was open for 6% of the time, Pallas kernels for 0%

profile of v1, /device:TPU:24, one launch (start us, length us, event | category | flops | bytes accessed | tf_op | source)
XLA Modules:
  0.0 462.7 jit_solution(4598111647328410270)
XLA Ops:
  6.5 0.0 copy-start
  6.5 0.0 copy-start.2
  6.5 0.0 copy-start.1
  6.5 0.0 all-gather.2.cloned.1.call-start
  6.5 1.1 fusion.31
  7.7 1.1 copy.15
  8.8 0.2 fusion.34
  9.0 10.5 %all-reduce = (f32[128]{0:T(128)S(1)}, f32[128]{0:T(128)S(1)}) all-reduce(f32[128]{0:T(128)S(1)} %fusion.34, f32[128]{0:T(128)S(1)} %fusion.31), channel_id=1, replica_groups=mesh['dp'=4,'ctx'=32,'tp'=4] {'tp'}, use_global_device_ids=true, to_apply=%region_3.0 | all-reduce | flops 256 | bytes 2048 | tf_op jit(solution)/shard_map/psum | solution.py:32
  19.5 0.9 fusion.36
  20.4 0.9 copy.16
  21.2 0.0 all-gather.2.cloned.1.call-update
  21.2 1.1 copy.21
  22.4 5.4 %stack.3 = bf16[32,128,8,128]{1,3,2,0:T(8,128)(2,1)} broadcast(bf16[128,8,128]{0,2,1:T(8,128)(2,1)S(1)} %bitcast.43), dimensions={1,2,3} | broadcast | bytes 8650752 | tf_op jit(solution)/shard_map/stack | solution.py:42
  27.7 16.0 %all-to-all-start = ((bf16[32,128,8,128]{1,3,2,0:T(8,128)(2,1)}), bf16[32,128,8,128]{1,3,2,0:T(8,128)(2,1)}, u32[]{:S(2)}, u32[]{:S(2)}) async-start(bf16[32,128,8,128]{1,3,2,0:T(8,128)(2,1)} %stack.3), calls=%async_computation | async-start | bytes 16777216 | tf_op jit(solution)/shard_map/all_to_all | solution.py:42
  43.7 0.0 copy-done.2
  43.8 0.1 broadcast_bitcast_fusion
  43.8 380.7 %all-gather.2.cloned.1.call-done = bf16[4096,8,128]{2,0,1:T(8,128)(2,1)} async-done(((bf16[128,8,128]{2,0,1:T(8,128)(2,1)}), bf16[4096,8,128]{2,0,1:T(8,128)(2,1)}) %all-gather.2.cloned.1.call-update) | async-done | bytes 8388624 | tf_op jit(solution)/shard_map/all_gather | solution.py:40
  424.6 0.0 copy-done
  424.6 0.0 copy-done.1
  424.6 11.6 %fusion = (f32[8,128]{1,0:T(8,128)S(1)}, f32[8,128,4096]{2,1,0:T(8,128)}) fusion(pred[4096]{0:T(1024)(128)(4,1)S(1)} %broadcast_bitcast_fusion, bf16[4096,8,128]{2,0,1:T(8,128)(2,1)} %all-gather.2.cloned.1.call-done, bf16[128,1024]{1,0:T(8,128)(2,1)S(1)} %copy-done, f32[1024]{0:T(1024)S(1)} %copy-done.1, f32[128]{0:T(128)S(1)} %add_rsqrt_fusion.1), kind=kOutput, calls=%fused_computation.2 | convolution fusion | flops 1086848000 | bytes 25440768 | tf_op jit(solution)/shard_map/qhd,khd->hqk/dot_general | solution.py:48
  436.2 8.3 %fusion.1 = f32[8,128]{1,0:T(8,128)S(1)} fusion(f32[8,128,4096]{2,1,0:T(8,128)} %get-tuple-element.10, f32[8,128]{1,0:T(8,128)S(1)} %get-tuple-element.8, pred[4096]{0:T(1024)(128)(4,1)S(1)} %broadcast_bitcast_fusion), kind=kLoop, calls=%fused_computation.3 | loop fusion | flops 20970496 | bytes 16789504 | tf_op jit(solution)/shard_map/reduce_sum | solution.py:55
  444.5 0.0 all-to-all-done
  444.5 10.5 %fusion.26 = bf16[128,8,128]{0,2,1:T(8,128)(2,1)S(1)} fusion(f32[8,128,4096]{2,1,0:T(8,128)} %get-tuple-element.10, f32[8,128]{1,0:T(8,128)S(1)} %get-tuple-element.8, pred[4096]{0:T(1024)(128)(4,1)S(1)} %broadcast_bitcast_fusion, f32[128,8]{0,1:T(8,128)S(1)} %bitcast.46, f32[128,8]{0,1:T(8,128)S(1)} %get-tuple-element.7, ...), kind=kOutput, calls=%fused_computation.15 | convolution fusion | flops 1095106560 | bytes 25444352 | tf_op jit(solution)/shard_map/hqk,khd->qhd/dot_general | solution.py:56
  455.0 0.9 copy.20
  (4 shorter events, 0.0 us)
Async XLA Ops:
  6.5 418.0 %copy-start = (bf16[128,1024]{1,0:T(8,128)(2,1)S(1)}, bf16[128,1024]{1,0:T(8,128)(2,1)}, u32[]{:S(2)}) copy-start(bf16[128,1024]{1,0:T(8,128)(2,1)} %param.6) | copy-start | bytes 786436
  6.5 37.2 %copy-start.2 = (s32[1,32]{1,0:T(1,128)S(1)}, s32[1,32]{1,0:T(1,128)}, u32[]{:S(2)}) copy-start(s32[1,32]{1,0:T(1,128)} %param.11) | copy-start | bytes 388
  6.5 418.0 %copy-start.1 = (f32[1024]{0:T(1024)S(1)}, f32[1024]{0:T(1024)}, u32[]{:S(2)}) copy-start(f32[1024]{0:T(1024)} %param.9) | copy-start | bytes 12292
  6.5 418.0 %all-gather.2.cloned.1.call-start = ((), (), s32[]{:S(2)}) async-start(), calls=%async_computation.1 | async-start | bytes 8650752 | tf_op jit(solution)/shard_map/all_gather | solution.py:40
  27.7 416.8 %all-to-all-start = ((bf16[32,128,8,128]{1,3,2,0:T(8,128)(2,1)}), bf16[32,128,8,128]{1,3,2,0:T(8,128)(2,1)}, u32[]{:S(2)}, u32[]{:S(2)}) async-start(bf16[32,128,8,128]{1,3,2,0:T(8,128)(2,1)} %stack.3), calls=%async_computation | async-start | bytes 16777216 | tf_op jit(solution)/shard_map/all_to_all | solution.py:42
Sparse Core Ops, SparseCore 0:
  21.4 403.1 all-gather.1
